TPU v7x, 32 devices: a whole 2x2x4 slice. The times are simulated.
32 devices in a mesh: shot: 4 (over z), slab: 8 (over y, x, core).
Axes of the slice: x: 2, y: 2, z: 4, core: 2. Of those that a mesh axis runs over, the one named last changes fastest.
Arguments:
- source_field: bfloat16 [4, 256, 384, 512], P('shot', 'slab'), may hold values from -6 to 6
- receiver_fields: bfloat16 [8, 256, 384, 512], P('shot', 'slab'), may hold values from -6 to 6
- weights: int32 [8], P('shot'), may hold values from -1 to 1, as said below
- model: bfloat16 [256, 384, 512], P(('slab', 'shot')), may hold values from -6 to 6
- wedge_sizes: int32 [16], replicated, may hold values from 1 to 95, as said below
- wedge_scales: float32 [16], replicated, may hold values from 0.3 to 3
Outputs:
- new_model: float32 [256, 384, 512], P(('slab', 'shot'))
Inputs may be any that keep to these rules, and one draw needn't show every extreme that they name: `weights`: each weight is -1 or +1. `wedge_sizes`: wedges 2d and 2d + 1 together hold either 512 // 8 // 2 or 96 columns, each count for half of the pairs; every wedge holds one column or more; all sizes sum to 512.
All inputs are finite; a program needn't handle non-finite values.
Results may differ from a plain program's by a relative error of at most 0.0003.
Values sent between devices are 32-bit elements; how exact they have to be, the bound alone decides.
A program may use at most 128 MiB of HBM per device.

v0:
```python
import jax
import jax.numpy as jnp
from jax import lax
from jax.sharding import PartitionSpec as P

STEP_SIZE = 0.25
EPSILON = 1e-06
HIGHEST = lax.Precision.HIGHEST


def dft_tables(length):
    counter = lax.iota(jnp.int32, length)
    phase = counter[:, None] * counter[None, :] % length
    angle = phase.astype(jnp.float32) * (2.0 * jnp.pi / length)
    return (jnp.cos(angle), jnp.sin(angle))


def complex_table(length, sign):
    cosine, sine = dft_tables(length)
    top = jnp.stack([cosine, -sign * sine], axis=0)
    bottom = jnp.stack([sign * sine, cosine], axis=0)
    return jnp.stack([top, bottom], axis=0)


def shrink_slots(received, slot_wedge, wedge_sizes, wedge_scales, live_slots, power_sum):
    depth = received.shape[0]
    forward = complex_table(depth, -1.0)
    inverse = complex_table(depth, 1.0)
    transformed = jnp.einsum("abjz,zcbq->jcaq", forward, received, precision=HIGHEST)
    energy = (
        transformed[:, :, 0] * transformed[:, :, 0] + transformed[:, :, 1] * transformed[:, :, 1]
    )
    column_power = jnp.sum(energy, axis=(0, 2))
    wedge_part = jnp.dot(column_power, slot_wedge, precision=HIGHEST)
    wedge_power = power_sum(wedge_part)
    entries = wedge_sizes.astype(jnp.float32) * (depth * received.shape[3] * lax.axis_size("shot"))
    spread = jnp.sqrt(wedge_power / entries + EPSILON)
    level = jnp.dot(slot_wedge, wedge_scales * spread, precision=HIGHEST)
    level = jnp.where(live_slots, level, 1.0)[None, :, None]
    magnitude = jnp.sqrt(energy)
    factor = jnp.maximum(magnitude - level, 0.0) / jnp.maximum(magnitude, level)
    kept = transformed * factor[:, :, None, :]
    return jnp.einsum("abzj,jcbq->zcaq", inverse, kept, precision=HIGHEST)


def on_device(source_field, receiver_fields, weights, model, wedge_sizes, wedge_scales):
    shots_local = receiver_fields.shape[0]
    planes = model.shape[0]
    signs = weights.astype(jnp.float32)
    source_rows = source_field[0].astype(jnp.float32)
    encoded = jnp.zeros(source_rows.shape, jnp.float32)
    for member in range(shots_local):
        encoded = encoded + signs[member] * receiver_fields[member].astype(jnp.float32)
    gradient = lax.psum_scatter(source_rows * encoded, "shot", scatter_dimension=0, tiled=True)
    update = model.astype(jnp.float32) - STEP_SIZE * gradient
    width_y = update.shape[1]
    width_x = update.shape[2]
    cos_x, sin_x = dft_tables(width_x)
    table_x = jnp.stack([cos_x, -sin_x], axis=0)
    forward_y = complex_table(width_y, -1.0)
    inverse_y = complex_table(width_y, 1.0)
    along_x = jnp.einsum("zyx,cxk->czyk", update, table_x, precision=HIGHEST)
    spectrum = jnp.einsum("abjy,bzyk->zkaj", forward_y, along_x, precision=HIGHEST)
    slab_count = lax.axis_size("slab")
    shot_count = lax.axis_size("shot")
    ky_local = width_y // shot_count
    ends = jnp.cumsum(wedge_sizes)
    starts = ends - wedge_sizes
    share = width_x // slab_count
    received = lax.all_to_all(
        lax.all_to_all(spectrum, "shot", split_axis=3, concat_axis=0, tiled=True),
        "slab",
        split_axis=1,
        concat_axis=0,
        tiled=True,
    )
    my_columns = lax.axis_index("slab") * share + lax.iota(jnp.int32, share)
    slot_wedge = (
        (my_columns[:, None] >= starts[None, :]) & (my_columns[:, None] < ends[None, :])
    ).astype(jnp.float32)
    every_slot = jnp.ones((share,), dtype=bool)
    shrunk = shrink_slots(
        received,
        slot_wedge,
        wedge_sizes,
        wedge_scales,
        every_slot,
        lambda part: lax.psum(part, ("shot", "slab")),
    )
    returned = lax.all_to_all(
        lax.all_to_all(
            shrunk.reshape(slab_count, shot_count, planes, share, 2, ky_local),
            "shot",
            split_axis=1,
            concat_axis=5,
            tiled=True,
        ),
        "slab",
        split_axis=0,
        concat_axis=3,
        tiled=True,
    )
    cleaned = returned.reshape(planes, width_x, 2, width_y)
    depth = received.shape[0]
    back_y = jnp.einsum("abyj,zkbj->azyk", inverse_y, cleaned, precision=HIGHEST)
    image = jnp.einsum("czyk,ckx->zyx", back_y, table_x, precision=HIGHEST)
    return image * (1.0 / (depth * width_y * width_x))


def solution(mesh):
    placed = (
        P("shot", "slab", None, None),
        P("shot", "slab", None, None),
        P("shot"),
        P(("slab", "shot"), None, None),
        P(),
        P(),
    )
    return jax.shard_map(
        on_device,
        mesh=mesh,
        in_specs=placed,
        out_specs=P(("slab", "shot"), None, None),
        check_vma=False,
    )
```

profile of v0, /device:TPU:0, one launch (start us, length us, event | category | flops | bytes accessed | tf_op | source)
XLA Modules:
  0.0 1873.3 jit_solution(2922640327999646719)
XLA Ops:
  6.5 0.0 reduce-scatter.2.cloned.1.call-start
  6.5 0.7 convert_element_type.107
  7.2 0.6 fusion.89
  7.8 22.8 %multiply_bitcast_fusion = f32[32,384,512]{2,1,0:T(8,128)} fusion(bf16[1,32,384,512]{3,2,1,0:T(8,128)(2,1)} %param.6, bf16[2,32,384,512]{3,2,1,0:T(8,128)(2,1)} %param.7, f32[]{:T(128)} %bitcast.2, f32[]{:T(128)} %bitcast.1), kind=kLoop, calls=%fused_computation | loop fusion | flops 44040192 | bytes 62914568 | tf_op jit(solution)/shard_map/mul | solution.py:54
  30.7 0.0 reduce-scatter.2.cloned.1.call-update
  30.7 2.3 broadcast_multiply_fusion
  33.0 2.4 fusion.52
  35.4 4.1 sine_negate_fusion
  39.5 2.1 fusion.37
  41.6 406.2 %reduce-scatter.2.cloned.1.call-done = f32[8,384,512]{2,1,0:T(8,128)} async-done(((f32[32,384,512]{2,1,0:T(8,128)}), f32[8,384,512]{2,1,0:T(8,128)}) %reduce-scatter.2.cloned.1.call-update) | async-done | bytes 6291472 | tf_op jit(solution)/shard_map/reduce_scatter | solution.py:54
  447.8 24.5 %fusion.10 = f32[2,512,8,384]{3,1,0,2:T(8,128)S(1)} fusion(f32[8,384,512]{2,1,0:T(8,128)} %reduce-scatter.2.cloned.1.call-done, bf16[8,384,512]{2,1,0:T(8,128)(2,1)} %param.9, f32[1,512,512]{1,2,0:T(8,128)S(1)} %get-tuple-element.19, f32[1,512,512]{1,2,0:T(8,128)S(1)} %get-tuple-element.20), kind=kOutput, calls=%fused_computation.13 | convolution fusion | flops 19332595712 | bytes 24117248 | tf_op jit(solution)/shard_map/zyx,cxk->czyk/dot_general | solution.py:62
  472.3 0.0 copy-done.2
  472.3 0.0 copy-done.4
  472.4 0.0 copy-done.8
  472.4 32.8 %fusion.16 = f32[8,512,2,384]{3,1,2,0:T(8,128)} fusion(f32[2,512,8,384]{3,1,0,2:T(8,128)S(1)} %fusion.10, f32[1,2,384,384]{3,2,1,0:T(8,128)S(1)} %get-tuple-element.6, f32[1,2,384,384]{3,2,1,0:T(8,128)S(1)} %copy-done.8), kind=kOutput, calls=%fused_computation.21 | convolution fusion | flops 28991619072 | bytes 27525120 | tf_op jit(solution)/shard_map/abjy,bzyk->zkaj/dot_general | solution.py:63
  505.1 19.1 %copy.17 = f32[8,512,2,384]{1,2,0,3:T(2,128)} copy(f32[8,512,2,384]{3,1,2,0:T(8,128)} %fusion.16) | data formatting | bytes 25165824 | tf_op jit(solution)/shard_map/abjy,bzyk->zkaj/dot_general | solution.py:63
  524.3 294.6 %all_to_all.69 = f32[8,512,2,384]{1,2,0,3:T(2,128)} all-to-all(f32[8,512,2,384]{1,2,0,3:T(2,128)} %copy.17), channel_id=1, replica_groups=mesh['shot'=4,'slab'=8] {'shot'}, dimensions={3} | all-to-all | bytes 25165824 | tf_op jit(solution)/shard_map/all_to_all | solution.py:71
  818.9 16.4 copy.18
  835.3 11.9 copy.19
  847.2 22.6 %copy.20 = f32[32,512,2,96]{3,2,0,1:T(2,128)} copy(f32[32,512,2,96]{1,3,2,0:T(8,128)} %bitcast.126) | data formatting | bytes 25165824 | tf_op jit(solution)/shard_map/all_to_all | solution.py:71
  869.7 5.9 all-to-all-start.1
  875.6 0.1 copy.24
  875.8 0.1 reduce.1
  875.9 1.0 fusion.67
  876.9 1.0 broadcast_multiply_fusion.1
  877.8 0.2 fusion.58
  878.0 181.5 %all-to-all-done.1 = f32[32,512,2,96]{3,2,0,1:T(2,128)} async-done(((f32[32,512,2,96]{3,2,0,1:T(2,128)}), f32[32,512,2,96]{3,2,0,1:T(2,128)}, u32[]{:S(2)}, u32[]{:S(2)}) %all-to-all-start.1) | async-done | bytes 12582944 | tf_op jit(solution)/shard_map/all_to_all | solution.py:70
  1059.5 11.0 copy.21
  1070.5 6.1 copy.22
  1076.6 64.5 %fusion.22 = f32[256,64,2,96]{0,3,2,1:T(8,128)S(1)} fusion(f32[256,64,2,96,1]{3,1,2,0,4:T(8,128)} %bitcast.122, f32[1,2,256,256]{3,2,1,0:T(8,128)S(1)} %get-tuple-element.12, f32[1,2,256,256]{3,2,1,0:T(8,128)S(1)} %get-tuple-element.15), kind=kOutput, calls=%fused_computation.23 | convolution fusion | flops 19327614976 | bytes 26214400 | tf_op jit(solution)/shard_map/abjz,zcbq->jcaq/dot_general | solution.py:29
  1141.1 0.0 copy-start.10
  1141.1 1.3 fusion.33
  1142.5 3.2 copy-done
  1145.6 0.2 convolution_bitcast_fusion.1
  1145.8 37.8 %psum.7 = f32[16]{0:T(128)S(1)} all-reduce(f32[16]{0:T(128)S(1)} %convolution_bitcast_fusion.1), channel_id=1, replica_groups=mesh['shot'=4,'slab'=8] {'shot','slab'}, use_global_device_ids=true, to_apply=%region_3.4 | all-reduce | flops 16 | bytes 128 | tf_op jit(solution)/shard_map/psum | solution.py:88
  1183.7 0.2 convolution_bitcast_fusion
  1183.9 6.4 divide_bitcast_fusion
  1190.3 1.8 copy-done.1
  1192.1 22.9 %fusion.19 = f32[256,64,2,96]{0,3,2,1:T(8,128)} fusion(f32[256,64,2,96]{0,3,2,1:T(8,128)S(1)} %copy-done.1, f32[256,64,96]{0,2,1:T(8,128)S(1)} %divide_bitcast_fusion, f32[1,2,256,256]{3,2,1,0:T(8,128)S(1)} %get-tuple-element.16, f32[1,2,256,256]{3,2,1,0:T(8,128)S(1)} %get-tuple-element.11), kind=kOutput, calls=%fused_computation.22 | convolution fusion | flops 19330760704 | bytes 32505856 | tf_op jit(solution)/shard_map/abzj,jcbq->zcaq/dot_general | solution.py:43
  1215.0 15.3 copy.25
  1230.3 6.6 copy.26
  1236.9 365.8 %all_to_all.70 = f32[8,4,8,64,2,96]{5,3,4,2,0,1:T(8,128)S(1)} all-to-all(f32[8,4,8,64,2,96]{5,3,4,2,0,1:T(8,128)S(1)} %copy.26), channel_id=1, replica_groups=mesh['shot'=4,'slab'=8] {'shot'}, dimensions={1} | all-to-all | bytes 25165824 | tf_op jit(solution)/shard_map/all_to_all | solution.py:91
  1602.6 12.0 copy.27
  1614.6 17.7 all_to_all.61
  1632.3 145.6 %all_to_all.71 = f32[8,1,8,64,2,384]{5,3,4,2,1,0:T(8,128)} all-to-all(f32[8,1,8,64,2,384]{5,3,4,2,1,0:T(8,128)} %bitcast.127), channel_id=1, replica_groups=mesh['shot'=4,'slab'=8] {'slab'}, dimensions={0} | all-to-all | bytes 25165824 | tf_op jit(solution)/shard_map/all_to_all | solution.py:90
  1777.9 11.0 copy.29
  1788.9 33.8 %fusion.30 = f32[8,512,2,384,1]{3,1,4,2,0:T(8,128)S(1)} fusion(f32[8,512,2,384,1]{3,1,2,4,0:T(8,128)} %bitcast.129, f32[1,2,384,384]{3,2,1,0:T(8,128)S(1)} %copy-done.7, f32[1,2,384,384]{3,2,1,0:T(8,128)S(1)} %copy-done.6), kind=kOutput, calls=%fused_computation.29 | convolution fusion | flops 28991619072 | bytes 27525120 | tf_op jit(solution)/shard_map/abyj,zkbj->azyk/dot_general | solution.py:105
  1822.7 43.5 %bitcast_multiply_fusion = f32[8,384,512]{2,1,0:T(8,128)} fusion(f32[8,512,2,384,1]{3,1,4,2,0:T(8,128)S(1)} %fusion.30, f32[1,512,512]{1,2,0:T(8,128)S(1)} %copy-done.3, f32[1,512,512]{1,2,0:T(8,128)S(1)} %copy-done.5), kind=kOutput, calls=%fused_computation.15 | convolution fusion | flops 19329449984 | bytes 20971520 | tf_op jit(solution)/shard_map/czyk,ckx->zyx/dot_general | solution.py:106
  (19 shorter events, 0.1 us)
Async XLA Ops:
  6.5 441.3 %reduce-scatter.2.cloned.1.call-start = ((), (), s32[]{:S(2)}) async-start(), calls=%async_computation.5 | async-start | bytes 31457280 | tf_op jit(solution)/shard_map/reduce_scatter | solution.py:54
  39.5 432.9 %copy-start.2 = (f32[1,512,512]{1,2,0:T(8,128)}, f32[1,512,512]{1,2,0:T(8,128)S(1)}, u32[]{:S(2)}) copy-start(f32[1,512,512]{1,2,0:T(8,128)S(1)} %get-tuple-element.19) | copy-start | bytes 3145732
  39.5 432.9 %copy-start.4 = (f32[1,512,512]{1,2,0:T(8,128)}, f32[1,512,512]{1,2,0:T(8,128)S(1)}, u32[]{:S(2)}) copy-start(f32[1,512,512]{1,2,0:T(8,128)S(1)} %get-tuple-element.20) | copy-start | bytes 3145732
  447.8 24.6 %copy-start.8 = (f32[1,2,384,384]{3,2,1,0:T(8,128)S(1)}, f32[1,2,384,384]{3,2,1,0:T(8,128)}, u32[]{:S(2)}) copy-start(f32[1,2,384,384]{3,2,1,0:T(8,128)} %get-tuple-element.9) | copy-start | bytes 3538948
  869.7 5.9 copy-start.9
  869.7 189.8 %all-to-all-start.1 = ((f32[32,512,2,96]{3,2,0,1:T(2,128)}), f32[32,512,2,96]{3,2,0,1:T(2,128)}, u32[]{:S(2)}, u32[]{:S(2)}) async-start(f32[32,512,2,96]{3,2,0,1:T(2,128)} %copy.20), calls=%async_computation.2 | async-start | bytes 33554432 | tf_op jit(solution)/shard_map/all_to_all | solution.py:70
  1141.1 4.5 copy-start
  1141.1 42.5 %copy-start.10 = (f32[16]{0:T(128)S(1)}, f32[16]{0:T(128)}, u32[]{:S(2)}) copy-start(f32[16]{0:T(128)} %param.11) | copy-start | bytes 196
  1183.9 8.3 copy-start.1
  1777.9 11.0 copy-start.6
  1777.9 11.0 copy-start.7
  1788.9 33.8 %copy-start.3 = (f32[1,512,512]{1,2,0:T(8,128)S(1)}, f32[1,512,512]{1,2,0:T(8,128)}, u32[]{:S(2)}) copy-start(f32[1,512,512]{1,2,0:T(8,128)} %copy-done.2) | copy-start | bytes 3145732
  1788.9 33.8 %copy-start.5 = (f32[1,512,512]{1,2,0:T(8,128)S(1)}, f32[1,512,512]{1,2,0:T(8,128)}, u32[]{:S(2)}) copy-start(f32[1,512,512]{1,2,0:T(8,128)} %copy-done.4) | copy-start | bytes 3145732
Sparse Core Ops, SparseCore 0:
  30.8 416.9 reduce-scatter.1
where the time goes:
time: 1880 us; the launch traced here: 1870 us
  blocking collectives  844 us (45%)
  waiting for transfers between devices  588 us (31%)
  matrix products  222 us (12%)
  local copies, waits for them, and re-layouts  155 us (8%)
  other arithmetic  44.4 us (2%)
    reduce_scatter x1, waiting for transfers between devices, on_device(): lax.psum_scatter(source_rows * encoded, 'shot', scatter_dimension=0, tile...  406 us
    all_to_all x1, blocking collectives, on_device(): lax.all_to_all(shrunk.reshape(slab_count, shot_count, planes, share, 2, k...  366 us
    all_to_all x1, blocking collectives, on_device(): lax.all_to_all(spectrum, 'shot', split_axis=3, concat_axis=0, tiled=True)  295 us
    all_to_all x1, waiting for transfers between devices, on_device(): lax.all_to_all(lax.all_to_all(spectrum, 'shot', split_axis=3, concat_axis...  182 us
    all_to_all x1, blocking collectives, on_device(): lax.all_to_all(lax.all_to_all(shrunk.reshape(slab_count, shot_count, plan...  146 us
    dot_general x1, matrix products, shrink_slots(): jnp.einsum('abjz,zcbq->jcaq', forward, received, precision=HIGHEST)  64.5 us
    all_to_all x3, local copies, waits for them, and re-layouts, on_device(): lax.all_to_all(spectrum, 'shot', split_axis=3, concat_axis=0, tiled=True)  50.8 us
    dot_general x1, matrix products, on_device(): image = jnp.einsum('czyk,ckx->zyx', back_y, table_x, precision=HIGHEST)  43.5 us
  transfers between devices with their start and end apart: 2, of which 2 were waited for; matrix products, arithmetic and copies ran while one was open for 1% of the time, Pallas kernels for 0%

commit v1 on v0

v1 whole, which is shorter than its diff:
```python
import functools

import jax
import jax.numpy as jnp
import numpy as np
from jax import lax
from jax.experimental import pallas as pl
from jax.experimental.pallas import tpu as pltpu
from jax.sharding import PartitionSpec as P

STEP_SIZE = 0.25
EPSILON = 1e-06
HIGHEST = lax.Precision.HIGHEST
CHUNKS = 4
F32 = jnp.float32
BF16 = jnp.bfloat16


def halves(x):
    high = x.astype(BF16)
    return high, (x - high.astype(F32)).astype(BF16)


def host_halves(table):
    table = table.astype(np.float32)
    high = table.astype(BF16)
    low = (table - high.astype(np.float32)).astype(BF16)
    return jnp.asarray(np.stack([high, low]))


def dot3(a, b, dims=((1,), (0,))):
    product = functools.partial(
        lax.dot_general, dimension_numbers=(dims, ((), ())), preferred_element_type=F32
    )
    return product(a[0], b[0]) + (product(a[0], b[1]) + product(a[1], b[0]))


def circle(rows, columns, length):
    angle = (np.outer(rows, columns) % length) * (2.0 * np.pi / length)
    return np.cos(angle), np.sin(angle)


def x_table(shots, slabs, width):
    slots = width // 2 // (shots * slabs)
    cosine, sine = circle(np.arange(width // 2), np.arange(width), width)
    sine = -sine
    sine[0] = 1.0 - 2.0 * (np.arange(width) % 2)
    shape = (shots * slabs, slots, width)
    return np.stack([cosine.reshape(shape), sine.reshape(shape)], axis=1).reshape(width, width)


def forward_x(shots, planes, first, sign_ref, shot_ref, source_ref, recv_ref, model_ref, tx_ref, out_ref):
    encoded = jnp.zeros(source_ref.shape[1:], F32)
    for member in range(recv_ref.shape[0]):
        encoded = encoded + sign_ref[member].astype(F32) * recv_ref[member, 0].astype(F32)
    plane = pl.program_id(0) + first
    own = (plane // planes == shot_ref[0]).astype(F32)
    part = own * model_ref[0].astype(F32) - STEP_SIZE * (source_ref[0].astype(F32) * encoded)
    result = dot3((tx_ref[0], tx_ref[1]), halves(part), ((1,), (1,)))
    rows = result.shape[0] // shots
    for shot in range(shots):
        out_ref[shot, 0] = result[shot * rows : (shot + 1) * rows]


def forward_y(slabs, in_ref, ty_ref, out_ref):
    depth, rows, width = in_ref.shape
    slots = rows // slabs // 2
    result = dot3(halves(in_ref[...].reshape(depth * rows, width)), (ty_ref[0], ty_ref[1]))
    with_cos, with_sin = result[:, :width], result[:, width:]
    for z in range(depth):
        for slab in range(slabs):
            re = z * rows + slab * 2 * slots
            im = re + slots
            out_ref[slab, z, 0] = with_cos[re : re + slots] + with_sin[im : im + slots]
            out_ref[slab, z, 1] = with_cos[im : im + slots] - with_sin[re : re + slots]


def forward_z(slots, packed_ref, tz_ref, *refs):
    pieces, (out_ref, middle_ref, power_ref) = refs[:CHUNKS], refs[CHUNKS:]
    slot = pl.program_id(0)
    depth = tz_ref.shape[2]

    def load(part):
        return jnp.concatenate([piece[part, 0] for piece in pieces], axis=0)

    def transform(re, im):
        width = re.shape[1]
        result = dot3((tz_ref[0], tz_ref[1]), halves(jnp.concatenate([re, im], axis=1)))
        with_cos, with_sin = result[:depth], result[depth:]
        return (
            with_cos[:, :width] + with_sin[:, width:],
            with_cos[:, width:] - with_sin[:, :width],
        )

    re_in, im_in = load(0), load(1)
    re, im = transform(re_in, im_in)
    out_ref[0, 0] = re
    out_ref[0, 1] = im
    power_ref[slot] = jnp.sum(re * re + im * im)

    @pl.when(slot == 0)
    def _():
        width = re.shape[1]
        sums = lax.broadcasted_iota(jnp.int32, (width, width), 0) + lax.broadcasted_iota(
            jnp.int32, (width, width), 1
        )
        mirror = ((sums == 0) | (sums == width)).astype(F32).astype(BF16)

        def flip(x):
            high, low = halves(x)
            return jnp.dot(high, mirror, preferred_element_type=F32) + jnp.dot(
                low, mirror, preferred_element_type=F32
            )

        other_re, other_im = transform(flip(re_in), -flip(im_in))
        flag = packed_ref[0] != 0
        first_re = jnp.where(flag, 0.5 * (re + other_re), re)
        first_im = jnp.where(flag, 0.5 * (im + other_im), im)
        last_re = jnp.where(flag, 0.5 * (im - other_im), 0.0)
        last_im = jnp.where(flag, 0.5 * (other_re - re), 0.0)
        out_ref[0, 0] = first_re
        out_ref[0, 1] = first_im
        middle_ref[0] = last_re
        middle_ref[1] = last_im
        power_ref[0] = jnp.sum(first_re * first_re + first_im * first_im)
        power_ref[slots] = jnp.sum(last_re * last_re + last_im * last_im)


def shrink_back(slots, level_ref, scale_ref, tz_ref, ty_ref, spec_ref, middle_ref, out_ref, held_ref):
    slot = pl.program_id(0)
    depth, width = spec_ref.shape[2:]

    def shrunk(re, im, index):
        magnitude = jnp.sqrt(re * re + im * im)
        total = 0.0
        for side in range(2):
            level = level_ref[side, index]
            total = total + jnp.maximum(magnitude - level, 0.0) / jnp.maximum(magnitude, level)
        total = total * scale_ref[index]
        return re * total, im * total

    re, im = shrunk(spec_ref[0, 0], spec_ref[0, 1], slot)
    held_ref[0] = re
    held_ref[1] = im

    @pl.when(slot == 0)
    def _():
        last_re, last_im = shrunk(middle_ref[0], middle_ref[1], slots)
        held_ref[0] = held_ref[0] - last_im
        held_ref[1] = held_ref[1] + last_re

    both = jnp.concatenate([held_ref[0], held_ref[1]], axis=1)
    result = dot3((tz_ref[0], tz_ref[1]), halves(both))
    with_cos, with_sin = result[:depth], result[depth:]
    re = with_cos[:, :width] - with_sin[:, width:]
    im = with_cos[:, width:] + with_sin[:, :width]
    result = dot3(halves(jnp.concatenate([re, im], axis=0)), (ty_ref[0], ty_ref[1]))
    with_cos, with_sin = result[:, :width], result[:, width:]
    owners, _, _, planes, _ = out_ref.shape
    re = with_cos[:depth] - with_sin[depth:]
    im = with_cos[depth:] + with_sin[:depth]
    out_ref[:, 0, 0] = re.reshape(owners, planes, width)
    out_ref[:, 1, 0] = im.reshape(owners, planes, width)


def inverse_x(in_ref, tx_ref, out_ref):
    out_ref[0] = dot3(halves(in_ref[0]), (tx_ref[0], tx_ref[1]), ((0,), (0,)))


def whole_block(array, memory_space=None):
    if memory_space is not None:
        return pl.BlockSpec(memory_space=memory_space)
    zeros = (0,) * array.ndim
    return pl.BlockSpec(array.shape, lambda *_: zeros)


def on_device(source_field, receiver_fields, weights, model, wedge_sizes, wedge_scales):
    shots = lax.axis_size("shot")
    slabs = lax.axis_size("slab")
    shot = lax.axis_index("shot")
    slab = lax.axis_index("slab")
    devices = shots * slabs
    members, local, height, width = receiver_fields.shape
    planes = model.shape[0]
    depth = local * slabs
    slots = width // 2 // devices
    rows = width // shots
    part = local // CHUNKS
    params = functools.partial(pltpu.CompilerParams, vmem_limit_bytes=60 * 1024 * 1024)

    tx = host_halves(x_table(shots, slabs, width))
    ty = host_halves(np.concatenate(circle(np.arange(height), np.arange(height), height), axis=1))
    chunk_order = np.arange(depth).reshape(slabs, CHUNKS, part).transpose(1, 0, 2).reshape(-1)
    owner_order = np.arange(depth).reshape(slabs, shots, planes).transpose(1, 0, 2).reshape(-1)
    wavenumbers = np.arange(depth)
    tz = host_halves(np.concatenate(circle(wavenumbers, chunk_order, depth), axis=0))
    tz_back = host_halves(np.concatenate(circle(owner_order, wavenumbers, depth), axis=0))

    shot_index = shot.astype(jnp.int32).reshape(1)
    received = []
    for chunk in range(CHUNKS):
        first = chunk * part

        def model_block(z, sign, own, first=first):
            return (jnp.clip(z + first - own[0] * planes, 0, planes - 1), 0, 0)

        along_x = pl.pallas_call(
            functools.partial(forward_x, shots, planes, first),
            out_shape=jax.ShapeDtypeStruct((shots, part, rows, height), F32),
            grid_spec=pltpu.PrefetchScalarGridSpec(
                num_scalar_prefetch=2,
                grid=(part,),
                in_specs=[
                    pl.BlockSpec((1, height, width), lambda z, *_, first=first: (z + first, 0, 0)),
                    pl.BlockSpec(
                        (members, 1, height, width), lambda z, *_, first=first: (0, z + first, 0, 0)
                    ),
                    pl.BlockSpec((1, height, width), model_block),
                    whole_block(tx),
                ],
                out_specs=pl.BlockSpec((shots, 1, rows, height), lambda z, *_: (0, z, 0, 0)),
            ),
            compiler_params=params(),
            cost_estimate=pl.CostEstimate(
                flops=6 * part * height * width * width,
                bytes_accessed=part * height * width * 12,
                transcendentals=0,
            ),
        )(weights, shot_index, source_field[0], receiver_fields, model, tx)
        summed = lax.psum_scatter(along_x, "shot", scatter_dimension=0, tiled=True)[0]
        batch = min(part, 4)
        along_y = pl.pallas_call(
            functools.partial(forward_y, slabs),
            out_shape=jax.ShapeDtypeStruct((slabs, part, 2, slots, height), F32),
            grid=(part // batch,),
            in_specs=[
                pl.BlockSpec((batch, rows, height), lambda z: (z, 0, 0)),
                whole_block(ty),
            ],
            out_specs=pl.BlockSpec(
                (slabs, batch, 2, slots, height), lambda z: (0, z, 0, 0, 0)
            ),
            compiler_params=params(),
            cost_estimate=pl.CostEstimate(
                flops=12 * part * rows * height * height,
                bytes_accessed=part * rows * height * 8,
                transcendentals=0,
            ),
        )(summed, ty)
        gathered = lax.all_to_all(along_y, "slab", split_axis=0, concat_axis=0, tiled=True)
        received.append(
            jnp.transpose(
                gathered.reshape(slabs * part, 2, slots, height), (1, 2, 0, 3)
            )
        )

    packed = ((shot == 0) & (slab == 0)).astype(jnp.int32).reshape(1)
    spectrum, middle, power = pl.pallas_call(
        functools.partial(forward_z, slots),
        out_shape=(
            jax.ShapeDtypeStruct((slots, 2, depth, height), F32),
            jax.ShapeDtypeStruct((2, depth, height), F32),
            jax.ShapeDtypeStruct((slots + 1,), F32),
        ),
        grid=(slots,),
        in_specs=[whole_block(packed, pltpu.SMEM), whole_block(tz)]
        + [
            pl.BlockSpec((2, 1, slabs * part, height), lambda k: (0, k, 0, 0))
            for _ in received
        ],
        out_specs=(
            pl.BlockSpec((1, 2, depth, height), lambda k: (k, 0, 0, 0)),
            pl.BlockSpec((2, depth, height), lambda k: (0, 0, 0)),
            pl.BlockSpec(memory_space=pltpu.SMEM),
        ),
        compiler_params=params(),
    )(packed, tz, *received)

    ends = jnp.cumsum(wedge_sizes)
    starts = ends - wedge_sizes

    def members_of(columns):
        return (
            (columns[:, None] >= starts[None, :]) & (columns[:, None] < ends[None, :])
        ).astype(F32)

    columns = (shot * slabs + slab) * slots + lax.iota(jnp.int32, slots)
    columns = jnp.concatenate([columns, jnp.full((1,), width // 2, jnp.int32)])
    paired = (width - columns) % width
    here, there = members_of(columns), members_of(paired)
    counted = here + jnp.where(paired == columns, 0.0, 1.0)[:, None] * there
    own_power = jnp.dot(power, counted, precision=HIGHEST)
    everywhere = jnp.broadcast_to(own_power[None, :], (devices, own_power.shape[0]))
    wedge_power = jnp.sum(
        lax.all_to_all(everywhere, ("shot", "slab"), split_axis=0, concat_axis=0, tiled=True), axis=0
    )
    entries = wedge_sizes.astype(F32) * (depth * height)
    heights = wedge_scales * jnp.sqrt(wedge_power / entries + EPSILON)
    levels = jnp.stack(
        [
            jnp.dot(here, heights, precision=HIGHEST),
            jnp.dot(there, heights, precision=HIGHEST),
        ]
    )
    scale = jnp.where(paired == columns, 0.5, 1.0) * (1.0 / (depth * height * width))

    returned = pl.pallas_call(
        functools.partial(shrink_back, slots),
        out_shape=jax.ShapeDtypeStruct((devices, 2, slots, planes, height), F32),
        grid=(slots,),
        in_specs=[
            whole_block(levels, pltpu.SMEM),
            whole_block(scale, pltpu.SMEM),
            whole_block(tz_back),
            whole_block(ty),
            pl.BlockSpec((1, 2, depth, height), lambda k: (k, 0, 0, 0)),
            whole_block(middle),
        ],
        out_specs=pl.BlockSpec((devices, 2, 1, planes, height), lambda k: (0, 0, k, 0, 0)),
        scratch_shapes=[pltpu.VMEM((2, depth, height), F32)],
        compiler_params=params(),
    )(levels, scale, tz_back, ty, spectrum, middle)

    cleaned = lax.all_to_all(
        returned, ("shot", "slab"), split_axis=0, concat_axis=0, tiled=True
    )
    cleaned = jnp.transpose(cleaned.reshape(width, planes, height), (1, 0, 2))
    return pl.pallas_call(
        inverse_x,
        out_shape=jax.ShapeDtypeStruct((planes, height, width), F32),
        grid=(planes,),
        in_specs=[
            pl.BlockSpec((1, width, height), lambda z: (z, 0, 0)),
            whole_block(tx),
        ],
        out_specs=pl.BlockSpec((1, height, width), lambda z: (z, 0, 0)),
        compiler_params=params(),
    )(cleaned, tx)


def solution(mesh):
    placed = (
        P("shot", "slab", None, None),
        P("shot", "slab", None, None),
        P("shot"),
        P(("slab", "shot"), None, None),
        P(),
        P(),
    )
    return jax.shard_map(
        on_device,
        mesh=mesh,
        in_specs=placed,
        out_specs=P(("slab", "shot"), None, None),
        check_vma=False,
    )
```

time: 1880 us -> 728 us (0.39)
  blocking collectives: 844 us -> 152 us
  matrix products: 222 us -> 1.14 us
  waiting for transfers between devices: 588 us -> 399 us
  local copies, waits for them, and re-layouts: 155 us -> 13.3 us
  Pallas kernels: 0 us -> 130 us
  other arithmetic: 44.4 us -> 1.6 us
    all_to_all x3 -> x2, blocking collectives: 806 us -> 152 us  [the longest x1 141 us: on_device(): lax.all_to_all(returned, ('shot', 'slab'), split_axis=0, concat_axis=0, t...]
    dot_general x8 -> x3, matrix products: 222 us -> 1.14 us  [the longest x1 0.77 us: on_device(): own_power = jnp.dot(power, counted, precision=HIGHEST)]
    all_to_all x1 -> x4, waiting for transfers between devices: 182 us -> 13.5 us  [on_device(): lax.all_to_all(along_y, 'slab', split_axis=0, concat_axis=0, tiled=True)]
    pallas_call x0 -> x11, Pallas kernels: none -> 130 us  [the longest x4 55.5 us: on_device(): pl.pallas_call(functools.partial(forward_x, shots, planes, first), out_sh...]
    all_to_all x8 -> x5, local copies, waits for them, and re-layouts: 108 us -> 13.2 us  [the longest x4 9.41 us: on_device(): lax.all_to_all(along_y, 'slab', split_axis=0, concat_axis=0, tiled=True)]
    psum x1 -> x0, blocking collectives: 37.8 us -> none  [on_device(): lax.psum(part, ('shot', 'slab'))]
    mul x4 -> x1, other arithmetic: 32.5 us -> 0.61 us  [on_device(): jnp.where(paired == columns, 0.5, 1.0) * (1.0 / (depth * height * width))]
    reduce_scatter x1 -> x4, waiting for transfers between devices: 406 us -> 386 us  [on_device(): lax.psum_scatter(along_x, 'shot', scatter_dimension=0, tiled=True)[0]]
  transfers between devices with their start and end apart: 2 -> 8, of which waited for: 2 -> 5; matrix products, arithmetic and copies ran while one was open for 1% -> 1% of each run, Pallas kernels for 0% -> 9%
where the time goes in v1:
time: 728 us; the launch traced here: 726 us
  waiting for transfers between devices  399 us (55%)
  blocking collectives  152 us (21%)
  Pallas kernels  130 us (18%)
  starting transfers between devices  16.4 us (2%)
  local copies, waits for them, and re-layouts  13.3 us (2%)
  between operations  13.2 us (2%)
    reduce_scatter x4, waiting for transfers between devices, on_device(): lax.psum_scatter(along_x, 'shot', scatter_dimension=0, tiled=True)[0]  386 us
    all_to_all x1, blocking collectives, on_device(): lax.all_to_all(returned, ('shot', 'slab'), split_axis=0, concat_axis=0, t...  141 us
    pallas_call x4, Pallas kernels, on_device(): pl.pallas_call(functools.partial(forward_x, shots, planes, first), out_sh...  55.5 us
    pallas_call x1, Pallas kernels, on_device(): pl.pallas_call(functools.partial(shrink_back, slots), out_shape=jax.Shape...  29.1 us
    pallas_call x4, Pallas kernels, on_device(): pl.pallas_call(functools.partial(forward_y, slabs), out_shape=jax.ShapeDt...  20.8 us
    all_to_all x4, starting transfers between devices, on_device(): lax.all_to_all(along_y, 'slab', split_axis=0, concat_axis=0, tiled=True)  16.2 us
  transfers between devices with their start and end apart: 8, of which 5 were waited for; matrix products, arithmetic and copies ran while one was open for 1% of the time, Pallas kernels for 9%

profile of v1, /device:TPU:0, one launch (start us, length us, event | category | flops | bytes accessed | tf_op | source)
XLA Modules:
  0.0 726.3 jit_solution(17909578366048750704)
XLA Ops:
  6.5 0.0 reduce-scatter.11.cloned.1.call-start
  6.5 13.7 %shard_map.106 = f32[4,8,128,384]{3,2,1,0:T(8,128)} custom-call(s32[2]{0:T(128)} %sign_ref.7, s32[1]{0:T(128)} %bitcast.2.shot_ref, bf16[32,384,512]{2,1,0:T(8,128)(2,1)} %bitcast.43, bf16[2,32,384,512]{3,2,1,0:T(8,128)(2,1)} %recv_ref.7, bf16[8,384,512]{2,1,0:T(8,128)(2,1)} %model_ref.7, bf16[2,512,512]{2,1,0:T(8,128)(2,1)} %constant.60.clone.tx_ref), custom_call_target="tpu_custom_call" | custom-call | flops 4831838208 | bytes 18874368 | tf_op jit(solution)/shard_map/pallas_call | solution.py:207
  20.3 0.0 reduce-scatter.11.cloned.1.call-update
  20.3 0.0 reduce-scatter.9.cloned.1.call-start
  20.3 13.9 %shard_map.104 = f32[4,8,128,384]{3,2,1,0:T(8,128)} custom-call(s32[2]{0:T(128)} %sign_ref.7, s32[1]{0:T(128)} %bitcast.2.shot_ref, bf16[32,384,512]{2,1,0:T(8,128)(2,1)} %bitcast.44, bf16[2,32,384,512]{3,2,1,0:T(8,128)(2,1)} %recv_ref.7, bf16[8,384,512]{2,1,0:T(8,128)(2,1)} %model_ref.7, bf16[2,512,512]{2,1,0:T(8,128)(2,1)} %constant.60.clone.tx_ref), custom_call_target="tpu_custom_call" | custom-call | flops 4831838208 | bytes 18874368 | tf_op jit(solution)/shard_map/pallas_call | solution.py:207
  34.2 0.0 reduce-scatter.9.cloned.1.call-update
  34.2 0.0 reduce-scatter.7.cloned.1.call-start
  34.3 13.8 %shard_map.102 = f32[4,8,128,384]{3,2,1,0:T(8,128)} custom-call(s32[2]{0:T(128)} %sign_ref.7, s32[1]{0:T(128)} %bitcast.2.shot_ref, bf16[32,384,512]{2,1,0:T(8,128)(2,1)} %bitcast.45, bf16[2,32,384,512]{3,2,1,0:T(8,128)(2,1)} %recv_ref.7, bf16[8,384,512]{2,1,0:T(8,128)(2,1)} %model_ref.7, bf16[2,512,512]{2,1,0:T(8,128)(2,1)} %constant.60.clone.tx_ref), custom_call_target="tpu_custom_call" | custom-call | flops 4831838208 | bytes 18874368 | tf_op jit(solution)/shard_map/pallas_call | solution.py:207
  48.0 0.0 reduce-scatter.7.cloned.1.call-update
  48.0 0.0 reduce-scatter.5.cloned.1.call-start
  48.1 14.1 %shard_map.100 = f32[4,8,128,384]{3,2,1,0:T(8,128)} custom-call(s32[2]{0:T(128)} %sign_ref.7, s32[1]{0:T(128)} %bitcast.2.shot_ref, bf16[32,384,512]{2,1,0:T(8,128)(2,1)} %bitcast.46, bf16[2,32,384,512]{3,2,1,0:T(8,128)(2,1)} %recv_ref.7, bf16[8,384,512]{2,1,0:T(8,128)(2,1)} %model_ref.7, bf16[2,512,512]{2,1,0:T(8,128)(2,1)} %constant.60.clone.tx_ref), custom_call_target="tpu_custom_call" | custom-call | flops 4831838208 | bytes 18874368 | tf_op jit(solution)/shard_map/pallas_call | solution.py:207
  62.2 0.0 reduce-scatter.5.cloned.1.call-update
  62.2 72.1 %reduce-scatter.11.cloned.1.call-done = f32[1,8,128,384]{3,2,1,0:T(8,128)} async-done(((f32[4,8,128,384]{3,2,1,0:T(8,128)}), f32[1,8,128,384]{3,2,1,0:T(8,128)}) %reduce-scatter.11.cloned.1.call-update) | async-done | bytes 1572880 | tf_op jit(solution)/shard_map/reduce_scatter | solution.py:230
  134.3 5.2 shard_map.107
  139.5 3.7 all-to-all-start.3
  143.2 104.7 %reduce-scatter.9.cloned.1.call-done = f32[1,8,128,384]{3,2,1,0:T(8,128)} async-done(((f32[4,8,128,384]{3,2,1,0:T(8,128)}), f32[1,8,128,384]{3,2,1,0:T(8,128)}) %reduce-scatter.9.cloned.1.call-update) | async-done | bytes 1572880 | tf_op jit(solution)/shard_map/reduce_scatter | solution.py:230
  247.9 5.2 shard_map.105
  253.1 0.0 all-to-all-done.3
  253.1 3.7 all-to-all-start.2
  256.8 104.8 %reduce-scatter.7.cloned.1.call-done = f32[1,8,128,384]{3,2,1,0:T(8,128)} async-done(((f32[4,8,128,384]{3,2,1,0:T(8,128)}), f32[1,8,128,384]{3,2,1,0:T(8,128)}) %reduce-scatter.7.cloned.1.call-update) | async-done | bytes 1572880 | tf_op jit(solution)/shard_map/reduce_scatter | solution.py:230
  361.6 5.2 shard_map.103
  366.7 0.0 all-to-all-done.2
  366.7 4.3 all-to-all-start.1
  371.0 104.0 %reduce-scatter.5.cloned.1.call-done = f32[1,8,128,384]{3,2,1,0:T(8,128)} async-done(((f32[4,8,128,384]{3,2,1,0:T(8,128)}), f32[1,8,128,384]{3,2,1,0:T(8,128)}) %reduce-scatter.5.cloned.1.call-update) | async-done | bytes 1572880 | tf_op jit(solution)/shard_map/reduce_scatter | solution.py:230
  475.0 5.2 shard_map.101
  480.2 0.0 all-to-all-done.1
  480.2 4.6 all-to-all-start
  484.8 0.1 copy.29
  485.0 0.1 reduce.1
  485.1 0.1 pad_add_fusion
  485.2 0.6 select_multiply_fusion
  485.8 0.1 broadcast_select_fusion
  485.9 1.6 copy.41
  487.5 1.6 copy.42
  489.1 3.1 copy.43
  492.2 13.5 %all-to-all-done = f32[8,8,2,8,384]{4,3,2,1,0:T(8,128)} async-done(((f32[8,8,2,8,384]{4,3,2,1,0:T(8,128)}), f32[8,8,2,8,384]{4,3,2,1,0:T(8,128)}, u32[]{:S(2)}, u32[]{:S(2)}) %all-to-all-start) | async-done | bytes 1572896 | tf_op jit(solution)/shard_map/all_to_all | solution.py:250
  505.6 3.1 copy.44
  508.7 13.7 %shard_map.108 = (f32[8,2,256,384]{3,2,1,0:T(8,128)}, f32[2,256,384]{2,1,0:T(8,128)}, f32[9]{0:T(128)}) custom-call(s32[1]{0:T(128)} %bitcast.1.packed_ref, bf16[2,512,256]{2,1,0:T(8,128)(2,1)} %constant.62.clone.tz_ref, f32[2,8,64,384]{3,2,1,0:T(8,128)} %bitcast.51, f32[2,8,64,384]{3,2,1,0:T(8,128)} %bitcast.50, f32[2,8,64,384]{3,2,1,0:T(8,128)} %bitcast.49, ...), custom_call_target="tpu_custom_call" | custom-call | tf_op jit(solution)/shard_map/pallas_call | solution.py:258
  522.5 0.8 convolution_bitcast_fusion
  523.3 10.3 %all_to_all.31 = f32[32,1,16]{2,1,0:T(1,128)S(1)} all-to-all(f32[32,1,16]{2,1,0:T(1,128)S(1)} %broadcast_in_dim.16), channel_id=1, replica_groups=mesh['shot'=4,'slab'=8] {'shot','slab'}, dimensions={0} | all-to-all | bytes 4096 | tf_op jit(solution)/shard_map/all_to_all | solution.py:295
  533.6 0.1 reduce_sum.9
  533.7 0.2 fusion.3
  533.8 0.2 fusion.4
  534.0 0.6 pad_maximum_fusion.level_ref
  534.6 29.1 %shard_map.109 = f32[32,2,8,8,384]{4,3,2,1,0:T(8,128)} custom-call(f32[2,9]{1,0:T(2,128)} %pad_maximum_fusion.level_ref, f32[9]{0:T(128)} %get-tuple-element.11.scale_ref, bf16[2,512,256]{2,1,0:T(8,128)(2,1)} %constant.63.clone.tz_ref, bf16[2,384,768]{2,1,0:T(8,128)(2,1)} %constant.61.clone.ty_ref, f32[8,2,256,384]{3,2,1,0:T(8,128)} %get-tuple-element.9.spec_ref, ...), custom_call_target="tpu_custom_call" | custom-call | tf_op jit(solution)/shard_map/pallas_call | solution.py:307
  563.7 141.4 %all_to_all.32 = f32[32,2,8,8,384]{4,3,2,1,0:T(8,128)S(1)} all-to-all(f32[32,2,8,8,384]{4,3,2,1,0:T(8,128)} %shard_map.109), channel_id=1, replica_groups=mesh['shot'=4,'slab'=8] {'shot','slab'}, dimensions={0} | all-to-all | bytes 12582912 | tf_op jit(solution)/shard_map/all_to_all | solution.py:324
  705.1 3.8 copy.35
  708.9 10.9 %shard_map.110 = f32[8,384,512]{2,1,0:T(8,128)} custom-call(f32[8,512,384]{2,1,0:T(8,128)} %bitcast.47, bf16[2,512,512]{2,1,0:T(8,128)(2,1)} %constant.60.clone.tx_ref), custom_call_target="tpu_custom_call" | custom-call | tf_op jit(solution)/shard_map/pallas_call | solution.py:328
  (8 shorter events, 0.1 us)
Async XLA Ops:
  6.5 127.8 %reduce-scatter.11.cloned.1.call-start = ((), (), s32[]{:S(2)}) async-start(), calls=%async_computation.13 | async-start | bytes 7864320 | tf_op jit(solution)/shard_map/reduce_scatter | solution.py:230
  20.3 227.7 %reduce-scatter.9.cloned.1.call-start = ((), (), s32[]{:S(2)}) async-start(), calls=%async_computation.12 | async-start | bytes 7864320 | tf_op jit(solution)/shard_map/reduce_scatter | solution.py:230
  34.2 327.3 %reduce-scatter.7.cloned.1.call-start = ((), (), s32[]{:S(2)}) async-start(), calls=%async_computation.11 | async-start | bytes 7864320 | tf_op jit(solution)/shard_map/reduce_scatter | solution.py:230
  48.0 427.0 %reduce-scatter.5.cloned.1.call-start = ((), (), s32[]{:S(2)}) async-start(), calls=%async_computation.10 | async-start | bytes 7864320 | tf_op jit(solution)/shard_map/reduce_scatter | solution.py:230
  139.5 113.6 %all-to-all-start.3 = ((f32[8,8,2,8,384]{4,3,2,1,0:T(8,128)}), f32[8,8,2,8,384]{4,3,2,1,0:T(8,128)S(1)}, u32[]{:S(2)}, u32[]{:S(2)}) async-start(f32[8,8,2,8,384]{4,3,2,1,0:T(8,128)} %shard_map.107), calls=%async_computation.7 | async-start | bytes 3145728 | tf_op jit(solution)/shard_map/all_to_all | solution.py:250
  253.1 113.6 %all-to-all-start.2 = ((f32[8,8,2,8,384]{4,3,2,1,0:T(8,128)}), f32[8,8,2,8,384]{4,3,2,1,0:T(8,128)S(1)}, u32[]{:S(2)}, u32[]{:S(2)}) async-start(f32[8,8,2,8,384]{4,3,2,1,0:T(8,128)} %shard_map.105), calls=%async_computation.5 | async-start | bytes 3145728 | tf_op jit(solution)/shard_map/all_to_all | solution.py:250
  366.7 113.5 %all-to-all-start.1 = ((f32[8,8,2,8,384]{4,3,2,1,0:T(8,128)}), f32[8,8,2,8,384]{4,3,2,1,0:T(8,128)}, u32[]{:S(2)}, u32[]{:S(2)}) async-start(f32[8,8,2,8,384]{4,3,2,1,0:T(8,128)} %shard_map.103), calls=%async_computation.3 | async-start | bytes 3145728 | tf_op jit(solution)/shard_map/all_to_all | solution.py:250
  480.2 4.6 copy-start
  480.2 25.4 %all-to-all-start = ((f32[8,8,2,8,384]{4,3,2,1,0:T(8,128)}), f32[8,8,2,8,384]{4,3,2,1,0:T(8,128)}, u32[]{:S(2)}, u32[]{:S(2)}) async-start(f32[8,8,2,8,384]{4,3,2,1,0:T(8,128)} %shard_map.101), calls=%async_computation.1 | async-start | bytes 3145728 | tf_op jit(solution)/shard_map/all_to_all | solution.py:250
  508.7 24.9 %copy-start.1 = (f32[16]{0:T(128)S(1)}, f32[16]{0:T(128)}, u32[]{:S(2)}) copy-start(f32[16]{0:T(128)} %param.15) | copy-start | bytes 196
Sparse Core Ops, SparseCore 0:
  20.4 113.8 reduce-scatter.10
  136.6 111.2 reduce-scatter.8
  250.2 111.2 reduce-scatter.6
  363.7 111.2 reduce-scatter.4

commit v2 on v1

--- a/solution.py
+++ b/solution.py
@@ -1,4 +1,5 @@
 import functools
+import math
 
 import jax
 import jax.numpy as jnp
@@ -11,7 +12,7 @@
 STEP_SIZE = 0.25
 EPSILON = 1e-06
 HIGHEST = lax.Precision.HIGHEST
-CHUNKS = 4
+CHUNKS = (1, 5, 2)
 F32 = jnp.float32
 BF16 = jnp.bfloat16
 
@@ -38,6 +39,13 @@
 def circle(rows, columns, length):
     angle = (np.outer(rows, columns) % length) * (2.0 * np.pi / length)
     return np.cos(angle), np.sin(angle)
+
+
+def device_halves(rows, columns, length, axis):
+    angle = (rows[:, None] * columns[None, :] % length).astype(F32) * (2.0 * np.pi / length)
+    table = jnp.concatenate([jnp.cos(angle), jnp.sin(angle)], axis=axis)
+    high = lax.reduce_precision(table, 8, 7)
+    return jnp.stack([high.astype(BF16), (table - high).astype(BF16)])
 
 
 def x_table(shots, slabs, width):
@@ -76,7 +84,8 @@
 
 
 def forward_z(slots, packed_ref, tz_ref, *refs):
-    pieces, (out_ref, middle_ref, power_ref) = refs[:CHUNKS], refs[CHUNKS:]
+    count = len(CHUNKS)
+    pieces, (out_ref, middle_ref, power_ref) = refs[:count], refs[count:]
     slot = pl.program_id(0)
     depth = tz_ref.shape[2]
 
@@ -126,8 +135,8 @@
         power_ref[slots] = jnp.sum(last_re * last_re + last_im * last_im)
 
 
-def shrink_back(slots, level_ref, scale_ref, tz_ref, ty_ref, spec_ref, middle_ref, out_ref, held_ref):
-    slot = pl.program_id(0)
+def shrink_back(low, slots, level_ref, scale_ref, tz_ref, ty_ref, spec_ref, middle_ref, out_ref, held_ref):
+    slot = pl.program_id(0) + low
     depth, width = spec_ref.shape[2:]
 
     def shrunk(re, im, index):
@@ -163,8 +172,12 @@
     out_ref[:, 1, 0] = im.reshape(owners, planes, width)
 
 
-def inverse_x(in_ref, tx_ref, out_ref):
-    out_ref[0] = dot3(halves(in_ref[0]), (tx_ref[0], tx_ref[1]), ((0,), (0,)))
+def inverse_x(*refs):
+    count = len(refs) // 2
+    total = 0.0
+    for in_ref, tx_ref in zip(refs[:count], refs[count : 2 * count]):
+        total = total + dot3(halves(in_ref[0]), (tx_ref[0], tx_ref[1]), ((0,), (0,)))
+    refs[-1][0] = total
 
 
 def whole_block(array, memory_space=None):
@@ -185,21 +198,21 @@
     depth = local * slabs
     slots = width // 2 // devices
     rows = width // shots
-    part = local // CHUNKS
+    parts = [local * share // sum(CHUNKS) for share in CHUNKS]
     params = functools.partial(pltpu.CompilerParams, vmem_limit_bytes=60 * 1024 * 1024)
 
     tx = host_halves(x_table(shots, slabs, width))
-    ty = host_halves(np.concatenate(circle(np.arange(height), np.arange(height), height), axis=1))
-    chunk_order = np.arange(depth).reshape(slabs, CHUNKS, part).transpose(1, 0, 2).reshape(-1)
-    owner_order = np.arange(depth).reshape(slabs, shots, planes).transpose(1, 0, 2).reshape(-1)
-    wavenumbers = np.arange(depth)
-    tz = host_halves(np.concatenate(circle(wavenumbers, chunk_order, depth), axis=0))
-    tz_back = host_halves(np.concatenate(circle(owner_order, wavenumbers, depth), axis=0))
+    firsts = [sum(parts[:chunk]) for chunk in range(len(parts))]
+    depth_index = np.arange(depth, dtype=np.int32)
+    by_slab = depth_index.reshape(slabs, local)
+    chunk_order = np.concatenate(
+        [by_slab[:, a : a + part].reshape(-1) for a, part in zip(firsts, parts)]
+    )
+    owner_order = depth_index.reshape(slabs, shots, planes).transpose(1, 0, 2).reshape(-1)
 
     shot_index = shot.astype(jnp.int32).reshape(1)
-    received = []
-    for chunk in range(CHUNKS):
-        first = chunk * part
+    received, sums = [], []
+    for chunk, (first, part) in enumerate(zip(firsts, parts)):
 
         def model_block(z, sign, own, first=first):
             return (jnp.clip(z + first - own[0] * planes, 0, planes - 1), 0, 0)
@@ -227,8 +240,18 @@
                 transcendentals=0,
             ),
         )(weights, shot_index, source_field[0], receiver_fields, model, tx)
-        summed = lax.psum_scatter(along_x, "shot", scatter_dimension=0, tiled=True)[0]
-        batch = min(part, 4)
+        along_x, shot_index = lax.optimization_barrier((along_x, shot_index))
+        if chunk == 0:
+            order = (np.arange(height, dtype=np.int32), depth_index, chunk_order, owner_order)
+            along_x, order = lax.optimization_barrier((along_x, order))
+            height_index, plain, by_chunk, by_owner = order
+            ty = device_halves(height_index, height_index, height, 1)
+            tz = device_halves(plain, by_chunk, depth, 0)
+            tz_back = device_halves(by_owner, plain, depth, 0)
+        sums.append(lax.psum_scatter(along_x, "shot", scatter_dimension=0, tiled=True)[0])
+
+    for part, summed in zip(parts, sums):
+        batch = math.gcd(part, 4)
         along_y = pl.pallas_call(
             functools.partial(forward_y, slabs),
             out_shape=jax.ShapeDtypeStruct((slabs, part, 2, slots, height), F32),
@@ -266,7 +289,7 @@
         in_specs=[whole_block(packed, pltpu.SMEM), whole_block(tz)]
         + [
             pl.BlockSpec((2, 1, slabs * part, height), lambda k: (0, k, 0, 0))
-            for _ in received
+            for part in parts
         ],
         out_specs=(
             pl.BlockSpec((1, 2, depth, height), lambda k: (k, 0, 0, 0)),
@@ -304,38 +327,51 @@
     )
     scale = jnp.where(paired == columns, 0.5, 1.0) * (1.0 / (depth * height * width))
 
-    returned = pl.pallas_call(
-        functools.partial(shrink_back, slots),
-        out_shape=jax.ShapeDtypeStruct((devices, 2, slots, planes, height), F32),
-        grid=(slots,),
-        in_specs=[
-            whole_block(levels, pltpu.SMEM),
-            whole_block(scale, pltpu.SMEM),
-            whole_block(tz_back),
-            whole_block(ty),
-            pl.BlockSpec((1, 2, depth, height), lambda k: (k, 0, 0, 0)),
-            whole_block(middle),
-        ],
-        out_specs=pl.BlockSpec((devices, 2, 1, planes, height), lambda k: (0, 0, k, 0, 0)),
-        scratch_shapes=[pltpu.VMEM((2, depth, height), F32)],
-        compiler_params=params(),
-    )(levels, scale, tz_back, ty, spectrum, middle)
-
-    cleaned = lax.all_to_all(
-        returned, ("shot", "slab"), split_axis=0, concat_axis=0, tiled=True
-    )
-    cleaned = jnp.transpose(cleaned.reshape(width, planes, height), (1, 0, 2))
+    cut = slots // 4
+    groups = [(0, cut), (cut, slots)] if cut else [(0, slots)]
+    tables = lax.optimization_barrier((tx, along_y))[0].reshape(2, devices, 2, slots, width)
+    cleaned, sides = [], []
+    for low, high in groups:
+        count = high - low
+        returned = pl.pallas_call(
+            functools.partial(shrink_back, low, slots),
+            out_shape=jax.ShapeDtypeStruct((devices, 2, count, planes, height), F32),
+            grid=(count,),
+            in_specs=[
+                whole_block(levels, pltpu.SMEM),
+                whole_block(scale, pltpu.SMEM),
+                whole_block(tz_back),
+                whole_block(ty),
+                pl.BlockSpec((1, 2, depth, height), lambda k, low=low: (k + low, 0, 0, 0)),
+                whole_block(middle),
+            ],
+            out_specs=pl.BlockSpec((devices, 2, 1, planes, height), lambda k: (0, 0, k, 0, 0)),
+            scratch_shapes=[pltpu.VMEM((2, depth, height), F32)],
+            compiler_params=params(),
+            cost_estimate=pl.CostEstimate(
+                flops=12 * count * depth * height * (depth + height),
+                bytes_accessed=count * depth * height * 16,
+                transcendentals=count * depth * height,
+            ),
+        )(levels, scale, tz_back, ty, spectrum, middle)
+        back = lax.all_to_all(
+            returned, ("shot", "slab"), split_axis=0, concat_axis=0, tiled=True
+        )
+        terms = devices * 2 * count
+        cleaned.append(jnp.transpose(back.reshape(terms, planes, height), (1, 0, 2)))
+        sides.append(tables[:, :, :, low:high].reshape(2, terms, width))
+
     return pl.pallas_call(
         inverse_x,
         out_shape=jax.ShapeDtypeStruct((planes, height, width), F32),
         grid=(planes,),
         in_specs=[
-            pl.BlockSpec((1, width, height), lambda z: (z, 0, 0)),
-            whole_block(tx),
-        ],
+            pl.BlockSpec((1,) + piece.shape[1:], lambda z: (z, 0, 0)) for piece in cleaned
+        ]
+        + [whole_block(side) for side in sides],
         out_specs=pl.BlockSpec((1, height, width), lambda z: (z, 0, 0)),
         compiler_params=params(),
-    )(cleaned, tx)
+    )(*cleaned, *sides)
 
 
 def solution(mesh):

time: 728 us -> 735 us (level)
  blocking collectives: 152 us -> 0 us
  waiting for transfers between devices: 399 us -> 537 us
  other arithmetic: 1.6 us -> 9.45 us
  local copies, waits for them, and re-layouts: 13.3 us -> 20.9 us
    all_to_all x2 -> x0, blocking collectives: 152 us -> none  [the longest x1 141 us: on_device(): lax.all_to_all(returned, ('shot', 'slab'), split_axis=0, concat_axis=0, t...]
    all_to_all x0 -> x3, waiting for transfers between devices: none -> 120 us  [the longest x2 114 us: on_device(): lax.all_to_all(returned, ('shot', 'slab'), split_axis=0, concat_axis=0, t...]
    all_to_all x4 -> x3, waiting for transfers between devices: 13.5 us -> 39 us  [on_device(): lax.all_to_all(along_y, 'slab', split_axis=0, concat_axis=0, tiled=True)]
    reshape x0 -> x6, local copies, waits for them, and re-layouts: none -> 14.9 us  [the longest x2 6.8 us: on_device(): back.reshape(terms, planes, height)]
    all_to_all x0 -> x3, starting transfers between devices: none -> 10.3 us  [the longest x2 6.49 us: on_device(): lax.all_to_all(returned, ('shot', 'slab'), split_axis=0, concat_axis=0, t...]
    reduce_scatter x4 -> x3, waiting for transfers between devices: 386 us -> 377 us  [on_device(): lax.psum_scatter(along_x, 'shot', scatter_dimension=0, tiled=True)[0]]
    all_to_all x4 -> x1, local copies, waits for them, and re-layouts: 9.41 us -> 1.73 us  [on_device(): lax.all_to_all(along_y, 'slab', split_axis=0, concat_axis=0, tiled=True)]
    all_to_all x4 -> x3, starting transfers between devices: 16.2 us -> 12.2 us  [on_device(): lax.all_to_all(along_y, 'slab', split_axis=0, concat_axis=0, tiled=True)]
  transfers between devices with their start and end apart: 8 -> 9, of which waited for: 5 -> 7; matrix products, arithmetic and copies ran while one was open for 1% -> 3% of each run, Pallas kernels for 9% -> 12%
where the time goes in v2:
time: 735 us; the launch traced here: 732 us
  waiting for transfers between devices  537 us (73%)
  Pallas kernels  128 us (17%)
  starting transfers between devices  22.6 us (3%)
  local copies, waits for them, and re-layouts  20.9 us (3%)
  between operations  13.3 us (2%)
  other arithmetic  9.45 us (1%)
    reduce_scatter x3, waiting for transfers between devices, on_device(): lax.psum_scatter(along_x, 'shot', scatter_dimension=0, tiled=True)[0]  377 us
    all_to_all x2, waiting for transfers between devices, on_device(): lax.all_to_all(returned, ('shot', 'slab'), split_axis=0, concat_axis=0, t...  114 us
    pallas_call x3, Pallas kernels, on_device(): pl.pallas_call(functools.partial(forward_x, shots, planes, first), out_sh...  52.4 us
    all_to_all x3, waiting for transfers between devices, on_device(): lax.all_to_all(along_y, 'slab', split_axis=0, concat_axis=0, tiled=True)  39 us
    pallas_call x2, Pallas kernels, on_device(): pl.pallas_call(functools.partial(shrink_back, low, slots), out_shape=jax....  31.9 us
    pallas_call x3, Pallas kernels, on_device(): pl.pallas_call(functools.partial(forward_y, slabs), out_shape=jax.ShapeDt...  18.4 us
  transfers between devices with their start and end apart: 9, of which 7 were waited for; matrix products, arithmetic and copies ran while one was open for 3% of the time, Pallas kernels for 12%

profile of v2, /device:TPU:0, one launch (start us, length us, event | category | flops | bytes accessed | tf_op | source)
XLA Modules:
  0.0 732.4 jit_solution(16166562916889587668)
XLA Ops:
  6.5 8.4 %shard_map.109 = f32[4,4,128,384]{3,2,1,0:T(8,128)} custom-call(s32[2]{0:T(128)} %sign_ref.5, s32[1]{0:T(128)} %bitcast.2.shot_ref, bf16[32,384,512]{2,1,0:T(8,128)(2,1)} %bitcast.54, bf16[2,32,384,512]{3,2,1,0:T(8,128)(2,1)} %recv_ref.5, bf16[8,384,512]{2,1,0:T(8,128)(2,1)} %model_ref.5, bf16[2,512,512]{2,1,0:T(8,128)(2,1)} %constant.96.clone.tx_ref), custom_call_target="tpu_custom_call" | custom-call | flops 2415919104 | bytes 9437184 | tf_op jit(solution)/shard_map/pallas_call | solution.py:220
  15.0 30.3 %shard_map.111 = f32[4,20,128,384]{3,2,1,0:T(8,128)} custom-call(s32[2]{0:T(128)} %sign_ref.5, s32[1]{0:T(128)} %bitcast.2.shot_ref, bf16[32,384,512]{2,1,0:T(8,128)(2,1)} %bitcast.55, bf16[2,32,384,512]{3,2,1,0:T(8,128)(2,1)} %recv_ref.5, bf16[8,384,512]{2,1,0:T(8,128)(2,1)} %model_ref.5, bf16[2,512,512]{2,1,0:T(8,128)(2,1)} %constant.96.clone.tx_ref), custom_call_target="tpu_custom_call" | custom-call | flops 12079595520 | bytes 47185920 | tf_op jit(solution)/shard_map/pallas_call | solution.py:220
  45.3 13.7 %shard_map.113 = f32[4,8,128,384]{3,2,1,0:T(8,128)} custom-call(s32[2]{0:T(128)} %sign_ref.5, s32[1]{0:T(128)} %bitcast.2.shot_ref, bf16[32,384,512]{2,1,0:T(8,128)(2,1)} %bitcast.56, bf16[2,32,384,512]{3,2,1,0:T(8,128)(2,1)} %recv_ref.5, bf16[8,384,512]{2,1,0:T(8,128)(2,1)} %model_ref.5, bf16[2,512,512]{2,1,0:T(8,128)(2,1)} %constant.96.clone.tx_ref), custom_call_target="tpu_custom_call" | custom-call | flops 4831838208 | bytes 18874368 | tf_op jit(solution)/shard_map/pallas_call | solution.py:220
  59.1 0.7 reduce-scatter.6.cloned.1.call-update
  59.8 2.4 cosine_bitcast_fusion
  62.3 0.2 reduce-precision_convert_fusion
  62.4 1.2 pad_maximum_fusion.1.ty_ref
  63.6 14.5 %reduce-scatter.4.cloned.1.call-done = f32[1,4,128,384]{3,2,1,0:T(8,128)} async-done(((f32[4,4,128,384]{3,2,1,0:T(8,128)}), f32[1,4,128,384]{3,2,1,0:T(8,128)}) %reduce-scatter.4.cloned.1.call-update) | async-done | bytes 786448 | tf_op jit(solution)/shard_map/reduce_scatter | solution.py:251
  78.1 3.8 shard_map.110
  81.9 3.7 all-to-all-start
  85.6 105.6 %reduce-scatter.8.cloned.1.call-done = f32[1,8,128,384]{3,2,1,0:T(8,128)} async-done(((f32[4,8,128,384]{3,2,1,0:T(8,128)}), f32[1,8,128,384]{3,2,1,0:T(8,128)}) %reduce-scatter.8.cloned.1.call-update) | async-done | bytes 1572880 | tf_op jit(solution)/shard_map/reduce_scatter | solution.py:251
  191.2 5.2 shard_map.114
  196.4 3.7 all-to-all-start.2
  200.0 256.7 %reduce-scatter.6.cloned.1.call-done = f32[1,20,128,384]{3,2,1,0:T(8,128)} async-done(((f32[4,20,128,384]{3,2,1,0:T(8,128)}), f32[1,20,128,384]{3,2,1,0:T(8,128)}) %reduce-scatter.6.cloned.1.call-update) | async-done | bytes 3932176 | tf_op jit(solution)/shard_map/reduce_scatter | solution.py:251
  456.7 9.4 %shard_map.112 = f32[8,20,2,8,384]{4,3,2,1,0:T(8,128)} custom-call(f32[20,128,384]{2,1,0:T(8,128)} %bitcast.68, bf16[2,384,768]{2,1,0:T(8,128)(2,1)} %pad_maximum_fusion.1.ty_ref), custom_call_target="tpu_custom_call" | custom-call | flops 4529848320 | bytes 7864320 | tf_op jit(solution)/shard_map/pallas_call | solution.py:255
  466.1 4.9 all-to-all-start.1
  471.1 0.1 reduce.1
  471.3 0.7 select_multiply_fusion
  472.0 2.1 cosine_bitcast_fusion.1
  474.1 0.2 reduce-precision_convert_fusion.1
  474.3 0.8 pad_maximum_fusion.3.tz_ref
  475.2 1.1 copy.56
  476.3 1.7 copy.55
  478.1 39.0 %all-to-all-done.1 = f32[8,20,2,8,384]{4,3,2,1,0:T(8,128)} async-done(((f32[8,20,2,8,384]{4,3,2,1,0:T(8,128)}), f32[8,20,2,8,384]{4,3,2,1,0:T(8,128)}, u32[]{:S(2)}, u32[]{:S(2)}) %all-to-all-start.1) | async-done | bytes 3932192 | tf_op jit(solution)/shard_map/all_to_all | solution.py:273
  517.1 5.2 copy.53
  522.3 13.4 %shard_map.115 = (f32[8,2,256,384]{3,2,1,0:T(8,128)}, f32[2,256,384]{2,1,0:T(8,128)}, f32[9]{0:T(128)}) custom-call(s32[1]{0:T(128)} %bitcast.1.packed_ref, bf16[2,512,256]{2,1,0:T(8,128)(2,1)} %pad_maximum_fusion.3.tz_ref, f32[2,8,32,384]{3,2,1,0:T(8,128)} %bitcast.66, f32[2,8,160,384]{3,2,1,0:T(8,128)} %bitcast.60, f32[2,8,64,384]{3,2,1,0:T(8,128)} %bitcast.62), custom_call_target="tpu_custom_call" | custom-call | tf_op jit(solution)/shard_map/pallas_call | solution.py:281
  535.8 0.8 convolution_bitcast_fusion
  536.6 0.6 broadcast_in_dim.14
  537.2 3.9 all-to-all-start.3
  541.1 0.8 pad_maximum_fusion.5.tz_ref
  541.9 6.3 all-to-all-done.3
  548.3 0.2 fusion.18
  548.5 0.2 fusion.17
  548.7 0.6 pad_maximum_fusion.6.level_ref
  549.3 9.6 %shard_map.116 = f32[32,2,2,8,384]{4,3,2,1,0:T(8,128)} custom-call(f32[2,9]{1,0:T(2,128)} %pad_maximum_fusion.6.level_ref, f32[9]{0:T(128)} %get-tuple-element.33.scale_ref, bf16[2,512,256]{2,1,0:T(8,128)(2,1)} %pad_maximum_fusion.5.tz_ref, bf16[2,384,768]{2,1,0:T(8,128)(2,1)} %pad_maximum_fusion.1.ty_ref, f32[8,2,256,384]{3,2,1,0:T(8,128)} %get-tuple-element.30.spec_ref, ...), custom_call_target="tpu_custom_call" | custom-call | flops 1509949440 | bytes 3145728 | tf_op jit(solution)/shard_map/pallas_call | solution.py:336
  558.9 2.9 all-to-all-start.4
  561.9 22.3 %shard_map.117 = f32[32,2,6,8,384]{4,3,2,1,0:T(8,128)} custom-call(f32[2,9]{1,0:T(2,128)} %pad_maximum_fusion.6.level_ref, f32[9]{0:T(128)} %get-tuple-element.33.scale_ref, bf16[2,512,256]{2,1,0:T(8,128)(2,1)} %pad_maximum_fusion.5.tz_ref, bf16[2,384,768]{2,1,0:T(8,128)(2,1)} %pad_maximum_fusion.1.ty_ref, f32[8,2,256,384]{3,2,1,0:T(8,128)} %get-tuple-element.30.spec_ref, ...), custom_call_target="tpu_custom_call" | custom-call | flops 4529848320 | bytes 9437184 | tf_op jit(solution)/shard_map/pallas_call | solution.py:336
  584.1 15.4 %all-to-all-done.4 = f32[32,2,2,8,384]{4,3,2,1,0:T(8,128)S(1)} async-done(((f32[32,2,2,8,384]{4,3,2,1,0:T(8,128)}), f32[32,2,2,8,384]{4,3,2,1,0:T(8,128)S(1)}, u32[]{:S(2)}, u32[]{:S(2)}) %all-to-all-start.4) | async-done | bytes 1572896 | tf_op jit(solution)/shard_map/all_to_all | solution.py:357
  599.5 3.6 all-to-all-start.5
  603.1 0.2 slice.8
  603.3 1.3 slice.9
  604.6 0.8 reshape.604.refs_2_
  605.4 2.0 copy.46
  607.4 1.0 copy.42.refs_3_
  608.4 1.4 copy.54
  609.8 98.4 %all-to-all-done.5 = f32[32,2,6,8,384]{4,3,2,1,0:T(8,128)} async-done(((f32[32,2,6,8,384]{4,3,2,1,0:T(8,128)}), f32[32,2,6,8,384]{4,3,2,1,0:T(8,128)}, u32[]{:S(2)}, u32[]{:S(2)}) %all-to-all-start.5) | async-done | bytes 4718624 | tf_op jit(solution)/shard_map/all_to_all | solution.py:357
  708.2 5.4 copy.52
  713.6 12.3 %shard_map.118 = f32[8,384,512]{2,1,0:T(8,128)} custom-call(f32[8,128,384]{2,1,0:T(8,128)} %bitcast.63, f32[8,384,384]{2,1,0:T(8,128)} %bitcast.59, bf16[2,128,512]{2,1,0:T(8,128)(2,1)} %reshape.604.refs_2_, bf16[2,384,512]{2,1,0:T(8,128)(2,1)} %copy.42.refs_3_), custom_call_target="tpu_custom_call" | custom-call | tf_op jit(solution)/shard_map/pallas_call | solution.py:364
  (26 shorter events, 0.5 us)
Async XLA Ops:
  6.5 71.6 %reduce-scatter.4.cloned.1.call-start = ((), (), s32[]{:S(2)}) async-start(), calls=%async_computation.9 | async-start | bytes 3932160 | tf_op jit(solution)/shard_map/reduce_scatter | solution.py:251
  15.0 176.2 %reduce-scatter.8.cloned.1.call-start = ((), (), s32[]{:S(2)}) async-start(), calls=%async_computation.11 | async-start | bytes 7864320 | tf_op jit(solution)/shard_map/reduce_scatter | solution.py:251
  59.1 397.6 %reduce-scatter.6.cloned.1.call-start = ((), (), s32[]{:S(2)}) async-start(), calls=%async_computation.10 | async-start | bytes 19660800 | tf_op jit(solution)/shard_map/reduce_scatter | solution.py:251
  81.9 114.4 %all-to-all-start = ((f32[8,4,2,8,384]{4,3,2,1,0:T(8,128)}), f32[8,4,2,8,384]{4,3,2,1,0:T(8,128)S(1)}, u32[]{:S(2)}, u32[]{:S(2)}) async-start(f32[8,4,2,8,384]{4,3,2,1,0:T(8,128)} %shard_map.110), calls=%async_computation.1 | async-start | bytes 1572864 | tf_op jit(solution)/shard_map/all_to_all | solution.py:273
  196.4 269.7 %all-to-all-start.2 = ((f32[8,8,2,8,384]{4,3,2,1,0:T(8,128)}), f32[8,8,2,8,384]{4,3,2,1,0:T(8,128)S(1)}, u32[]{:S(2)}, u32[]{:S(2)}) async-start(f32[8,8,2,8,384]{4,3,2,1,0:T(8,128)} %shard_map.114), calls=%async_computation.5 | async-start | bytes 3145728 | tf_op jit(solution)/shard_map/all_to_all | solution.py:273
  466.1 4.9 copy-start.3
  466.1 5.9 copy-start.1
  466.1 5.9 copy-start.2
  466.1 51.0 %all-to-all-start.1 = ((f32[8,20,2,8,384]{4,3,2,1,0:T(8,128)}), f32[8,20,2,8,384]{4,3,2,1,0:T(8,128)}, u32[]{:S(2)}, u32[]{:S(2)}) async-start(f32[8,20,2,8,384]{4,3,2,1,0:T(8,128)} %shard_map.112), calls=%async_computation.3 | async-start | bytes 7864320 | tf_op jit(solution)/shard_map/all_to_all | solution.py:273
  522.3 26.0 %copy-start.4 = (f32[16]{0:T(128)S(1)}, f32[16]{0:T(128)}, u32[]{:S(2)}) copy-start(f32[16]{0:T(128)} %param.16) | copy-start | bytes 196
  537.2 11.0 %all-to-all-start.3 = ((f32[32,1,16]{2,1,0:T(1,128)}), f32[32,1,16]{2,1,0:T(1,128)S(1)}, u32[]{:S(2)}, u32[]{:S(2)}) async-start(f32[32,1,16]{2,1,0:T(1,128)} %broadcast_in_dim.14), calls=%async_computation.6 | async-start | bytes 32768 | tf_op jit(solution)/shard_map/all_to_all | solution.py:318
  558.9 40.6 %all-to-all-start.4 = ((f32[32,2,2,8,384]{4,3,2,1,0:T(8,128)}), f32[32,2,2,8,384]{4,3,2,1,0:T(8,128)S(1)}, u32[]{:S(2)}, u32[]{:S(2)}) async-start(f32[32,2,2,8,384]{4,3,2,1,0:T(8,128)} %shard_map.116), calls=%async_computation.7 | async-start | bytes 3145728 | tf_op jit(solution)/shard_map/all_to_all | solution.py:357
  584.1 19.0 %copy-start = (bf16[2,512,512]{2,1,0:T(8,128)(2,1)S(1)}, bf16[2,512,512]{2,1,0:T(8,128)(2,1)}, u32[]{:S(2)}) copy-start(bf16[2,512,512]{2,1,0:T(8,128)(2,1)} %constant.96.clone.tx_ref) | copy-start | bytes 3145732
  599.5 108.7 %all-to-all-start.5 = ((f32[32,2,6,8,384]{4,3,2,1,0:T(8,128)}), f32[32,2,6,8,384]{4,3,2,1,0:T(8,128)}, u32[]{:S(2)}, u32[]{:S(2)}) async-start(f32[32,2,6,8,384]{4,3,2,1,0:T(8,128)} %shard_map.117), calls=%async_computation.8 | async-start | bytes 9437184 | tf_op jit(solution)/shard_map/all_to_all | solution.py:357
Sparse Core Ops, SparseCore 0:
  15.1 62.9 reduce-scatter.3
  80.4 110.6 reduce-scatter.7
  193.5 263.1 reduce-scatter.5
